TPU v7x, 1024 devices: a whole 4x4x32 slice. The times are simulated.
1024 devices in a mesh: fsdp: 16 (over y, x), tp: 8 (over z_hi, core), ad: 8 (over z_lo).
Axes of the slice: x: 4, y: 4, z: 32 (z_hi: 4, z_lo: 8; z = z_hi * 8 + z_lo), core: 2. Of those that a mesh axis runs over, the one named last changes fastest.
Arguments:
- input_rows: bfloat16 [32768, 8192], P(('fsdp', 'ad')), may hold values from -6 to 6
- value_weight_frozen: bfloat16 [8192, 1024], P('fsdp', 'tp'), may hold values from -0.0625 to 0.0625
- adapter_down_weight: bfloat16 [32, 256, 8192], P('ad', None, 'tp'), may hold values from -0.0625 to 0.0625
- adapter_up_weight: bfloat16 [32, 256, 1024], P('ad', None, 'tp'), may hold values from -0.375 to 0.375
- layer_output_gradient: bfloat16 [32768, 1024], P(('fsdp', 'ad'), 'tp'), may hold values from -0.5 to 0.5
- domain: int32 [32768, 1], P(('fsdp', 'ad')), may hold values from 0 to 31; in each aligned block of 256 rows (0 to 255, 256 to 511, ...) at most 12 rows name the same one
Outputs:
- y_out: bfloat16 [32768, 1024], P(('fsdp', 'ad'), 'tp')
- grad_a: float32 [32, 256, 8192], P('ad', 'fsdp', 'tp')
- grad_b: float32 [32, 256, 1024], P('ad', 'fsdp', 'tp')
Inputs may be any that keep to these rules, and one draw needn't show every extreme that they name: In each aligned block of 256 rows (the tokens of one fsdp and ad index) no domain is named by more than 12 tokens, a bound that some block reaches.
All inputs are finite; a program needn't handle non-finite values.
Results may differ from a plain program's by a relative error of at most 0.004.
Values may be sent and summed in bfloat16 or wider, within the bound.
A program may use at most 64 MiB of HBM per device.

v0:
```python
import jax
import jax.numpy as jnp
from jax import lax
from jax.sharding import PartitionSpec as P

CAPD = 12


adapter_scale = 0.5


def body(
    input_rows,
    value_weight_frozen,
    adapter_down_weight,
    adapter_up_weight,
    layer_output_gradient,
    domain,
):
    row_count = input_rows.shape[0]
    domain_local = adapter_down_weight.shape[0]
    width_local = adapter_down_weight.shape[2]
    value_width_local = adapter_up_weight.shape[2]
    ad_count = lax.axis_size("ad")
    dom_total = ad_count * domain_local
    slot_total = dom_total * CAPD
    dom_ids = domain[:, 0]
    onehot = (dom_ids[:, None] == jnp.arange(dom_total, dtype=jnp.int32)[None, :]).astype(
        jnp.float32
    )
    row_iota = jnp.arange(row_count, dtype=jnp.int32)
    earlier = (row_iota[:, None] > row_iota[None, :]).astype(jnp.float32)
    prior = jnp.dot(earlier, onehot, preferred_element_type=jnp.float32)
    position = jnp.sum(prior * onehot, axis=1).astype(jnp.int32)
    place = dom_ids * CAPD + position
    matches = place[None, :] == jnp.arange(slot_total, dtype=jnp.int32)[:, None]
    filled = jnp.any(matches, axis=1)
    source_row = jnp.sum(jnp.where(matches, row_iota[None, :], 0), axis=1)
    base = jnp.dot(
        input_rows,
        lax.all_gather(value_weight_frozen, "fsdp", axis=0, tiled=True),
        preferred_element_type=jnp.float32,
    )
    feature_cols = lax.dynamic_slice_in_dim(
        input_rows, lax.axis_index("tp") * width_local, width_local, 1
    )
    zero_value = jnp.zeros((), jnp.bfloat16)
    send_x = jnp.where(filled[:, None], feature_cols[source_row], zero_value)
    send_dy = jnp.where(filled[:, None], layer_output_gradient[source_row], zero_value)
    send_x = send_x.reshape(ad_count, domain_local * CAPD, width_local)
    send_dy = send_dy.reshape(ad_count, domain_local * CAPD, value_width_local)
    got_x = lax.all_to_all(send_x, "ad", split_axis=0, concat_axis=0, tiled=True)
    got_dy = lax.all_to_all(send_dy, "ad", split_axis=0, concat_axis=0, tiled=True)
    routed_input_rows = got_x.reshape(ad_count, domain_local, CAPD, width_local)
    routed_output_gradient = got_dy.reshape(ad_count, domain_local, CAPD, value_width_local)
    hidden_partial = jnp.einsum(
        "vqfj,qwj->vqfw", routed_input_rows, adapter_down_weight, preferred_element_type=jnp.float32
    )
    input_gradient_partial = jnp.einsum(
        "amgy,mzy->amgz",
        routed_output_gradient,
        adapter_up_weight,
        preferred_element_type=jnp.float32,
    )
    hidden_sum, input_gradient_total = lax.psum((hidden_partial, input_gradient_partial), "tp")
    hidden_lowrank = hidden_sum.astype(jnp.bfloat16)
    input_gradient_lowrank = (adapter_scale * input_gradient_total).astype(jnp.bfloat16)
    adapter_update = adapter_scale * jnp.einsum(
        "lokh,ohi->loki", hidden_lowrank, adapter_up_weight, preferred_element_type=jnp.float32
    )
    adapter_update = adapter_update.astype(jnp.bfloat16).reshape(
        ad_count, domain_local * CAPD, value_width_local
    )
    part_a = jnp.einsum(
        "sdcr,sdcx->drx",
        input_gradient_lowrank,
        routed_input_rows,
        preferred_element_type=jnp.float32,
    )
    up_weight_partial = adapter_scale * jnp.einsum(
        "sdcr,sdce->dre", hidden_lowrank, routed_output_gradient, preferred_element_type=jnp.float32
    )
    returned = lax.all_to_all(
        adapter_update, "ad", split_axis=0, concat_axis=0, tiled=True
    ).reshape(slot_total, value_width_local)
    y_out = (base + returned[place].astype(jnp.float32)).astype(jnp.bfloat16)
    grad_a, grad_b = (
        lax.psum_scatter(part_a, "fsdp", scatter_dimension=1, tiled=True),
        lax.psum_scatter(up_weight_partial, "fsdp", scatter_dimension=1, tiled=True),
    )
    return (y_out, grad_a, grad_b)


def solution(mesh):
    placed = (
        P(("fsdp", "ad"), None),
        P("fsdp", "tp"),
        P("ad", None, "tp"),
        P("ad", None, "tp"),
        P(("fsdp", "ad"), "tp"),
        P(("fsdp", "ad"), None),
    )
    return jax.shard_map(
        body,
        mesh=mesh,
        in_specs=placed,
        out_specs=(P(("fsdp", "ad"), "tp"), P("ad", "fsdp", "tp"), P("ad", "fsdp", "tp")),
        check_vma=False,
    )
```

profile of v0, /device:TPU:33, one launch (start us, length us, event | category | flops | bytes accessed | tf_op | source)
XLA Modules:
  0.0 408.0 jit_solution(7778815511374388373)
XLA Ops:
  8.0 0.0 copy-start
  8.0 1.0 fusion.9
  9.1 0.7 multiply_add_fusion
  9.7 0.2 fusion.12
  9.9 0.2 select_reduce_fusion
  10.1 0.1 broadcast_in_dim.49
  10.2 2.0 gather_fusion.2
  12.2 0.8 broadcast_select_fusion.1
  13.0 12.1 %all-to-all-start.2 = ((bf16[8,48,128]{2,1,0:T(8,128)(2,1)}), bf16[8,48,128]{2,1,0:T(8,128)(2,1)S(1)}, u32[]{:S(2)}, u32[]{:S(2)}) async-start(bf16[8,48,128]{2,1,0:T(8,128)(2,1)} %broadcast_select_fusion.1), calls=%async_computation.2 | async-start | bytes 196608 | tf_op jit(solution)/shard_map/all_to_all | solution.py:53
  25.0 1.1 constant_dynamic-slice_fusion
  26.1 2.1 gather_fusion
  28.2 0.0 copy-start.1
  28.2 1.0 broadcast_select_fusion
  29.2 4.4 %all-to-all-done.2 = bf16[8,48,128]{2,1,0:T(8,128)(2,1)S(1)} async-done(((bf16[8,48,128]{2,1,0:T(8,128)(2,1)}), bf16[8,48,128]{2,1,0:T(8,128)(2,1)S(1)}, u32[]{:S(2)}, u32[]{:S(2)}) %all-to-all-start.2) | async-done | bytes 98336 | tf_op jit(solution)/shard_map/all_to_all | solution.py:53
  33.6 0.0 copy-start.4
  33.6 5.5 %all-to-all-start = ((bf16[8,48,1024]{2,1,0:T(8,128)(2,1)}), bf16[8,48,1024]{2,1,0:T(8,128)(2,1)}, u32[]{:S(2)}, u32[]{:S(2)}) async-start(bf16[8,48,1024]{2,1,0:T(8,128)(2,1)} %broadcast_select_fusion), calls=%async_computation | async-start | bytes 1572864 | tf_op jit(solution)/shard_map/all_to_all | solution.py:52
  39.1 0.0 copy-done.4
  39.2 0.0 all-reduce.3.cloned.1.call-start
  39.2 0.9 copy.38
  40.1 0.0 copy-done.1
  40.1 1.0 convolution_bitcast_fusion.2
  41.1 0.0 all-reduce.3.cloned.1.call-update
  41.2 0.0 all-gather.2.cloned.1.call-start
  41.2 0.5 all-gather.2.cloned.1.call-update
  41.7 0.0 reduce-scatter.5.cloned.1.call-start
  41.8 32.2 %all-to-all-done = bf16[8,48,1024]{2,1,0:T(8,128)(2,1)} async-done(((bf16[8,48,1024]{2,1,0:T(8,128)(2,1)}), bf16[8,48,1024]{2,1,0:T(8,128)(2,1)}, u32[]{:S(2)}, u32[]{:S(2)}) %all-to-all-start) | async-done | bytes 786464 | tf_op jit(solution)/shard_map/all_to_all | solution.py:52
  74.0 1.6 copy.34
  75.6 0.0 copy-done
  75.6 0.8 fusion.2
  76.4 97.4 %all-reduce.4 = bf16[8,4,12,256]{3,2,0,1:T(8,128)(2,1)} all-reduce(f32[8,4,12,256]{3,2,0,1:T(8,128)S(1)} %fusion.2), channel_id=1, replica_groups=mesh['fsdp'=16,'tp'=8,'ad'=8] {'tp'}, use_global_device_ids=true, to_apply=%region_3.4 | all-reduce | flops 98304 | bytes 589824 | tf_op jit(solution)/shard_map/psum | solution.py:65
  173.8 2.1 fusion.5
  175.9 0.0 reduce-scatter.5.cloned.1.call-update
  175.9 0.0 reduce-scatter.3.cloned.1.call-start
  176.0 45.6 %all-reduce.3.cloned.1.call-done = f32[8,4,12,256]{3,2,0,1:T(8,128)} async-done(((f32[8,4,12,256]{3,2,0,1:T(8,128)}), f32[8,4,12,256]{3,2,0,1:T(8,128)}) %all-reduce.3.cloned.1.call-update) | async-done | bytes 393232 | tf_op jit(solution)/shard_map/psum | solution.py:65
  221.6 3.8 convolution_bitcast_fusion
  225.3 0.0 reduce-scatter.3.cloned.1.call-update
  225.4 0.9 copy-done.2
  226.3 0.1 copy-done.3
  226.4 0.2 fusion.7
  226.6 0.7 copy.37
  227.3 9.0 %all-to-all-start.1 = ((bf16[8,48,128]{2,1,0:T(8,128)(2,1)}), bf16[8,48,128]{2,1,0:T(8,128)(2,1)S(1)}, u32[]{:S(2)}, u32[]{:S(2)}) async-start(bf16[8,48,128]{2,1,0:T(8,128)(2,1)} %copy.37), calls=%async_computation.1 | async-start | bytes 196608 | tf_op jit(solution)/shard_map/all_to_all | solution.py:83
  236.3 0.0 copy-done.5
  236.3 8.5 %all-to-all-done.1 = bf16[8,48,128]{2,1,0:T(8,128)(2,1)S(1)} async-done(((bf16[8,48,128]{2,1,0:T(8,128)(2,1)}), bf16[8,48,128]{2,1,0:T(8,128)(2,1)S(1)}, u32[]{:S(2)}, u32[]{:S(2)}) %all-to-all-start.1) | async-done | bytes 98336 | tf_op jit(solution)/shard_map/all_to_all | solution.py:83
  244.9 0.9 gather_fusion.1
  245.7 0.0 all-gather.2.cloned.1.call-done
  245.7 4.7 %fusion.8 = bf16[256,128]{1,0:T(8,128)(2,1)} fusion(bf16[256,8192]{1,0:T(8,128)(2,1)} %param.6, bf16[8192,128]{1,0:T(8,128)(2,1)} %all-gather.2.cloned.1.call-done, bf16[256,128]{1,0:T(8,128)(2,1)S(1)} %gather_fusion.1), kind=kOutput, calls=%fused_computation.14 | convolution fusion | flops 536969216 | bytes 6422528 | tf_op jit(solution)/shard_map/dot_general | solution.py:39
  250.5 30.7 %reduce-scatter.5.cloned.1.call-done = f32[4,16,128]{2,1,0:T(8,128)} async-done(((f32[4,256,128]{2,1,0:T(8,128)}), f32[4,16,128]{2,1,0:T(8,128)}) %reduce-scatter.5.cloned.1.call-update) | async-done | bytes 32784 | tf_op jit(solution)/shard_map/reduce_scatter | solution.py:89
  281.2 119.2 %reduce-scatter.3.cloned.1.call-done = f32[4,16,1024]{2,1,0:T(8,128)} async-done(((f32[4,256,1024]{2,1,0:T(8,128)}), f32[4,16,1024]{2,1,0:T(8,128)}) %reduce-scatter.3.cloned.1.call-update) | async-done | bytes 262160 | tf_op jit(solution)/shard_map/reduce_scatter | solution.py:88
  (9 shorter events, 0.1 us)
Async XLA Ops:
  8.0 67.6 %copy-start = (bf16[4,256,1024]{2,1,0:T(8,128)(2,1)S(1)}, bf16[4,256,1024]{2,1,0:T(8,128)(2,1)}, u32[]{:S(2)}) copy-start(bf16[4,256,1024]{2,1,0:T(8,128)(2,1)} %param.8) | copy-start | bytes 6291460
  13.0 20.6 %all-to-all-start.2 = ((bf16[8,48,128]{2,1,0:T(8,128)(2,1)}), bf16[8,48,128]{2,1,0:T(8,128)(2,1)S(1)}, u32[]{:S(2)}, u32[]{:S(2)}) async-start(bf16[8,48,128]{2,1,0:T(8,128)(2,1)} %broadcast_select_fusion.1), calls=%async_computation.2 | async-start | bytes 196608 | tf_op jit(solution)/shard_map/all_to_all | solution.py:53
  28.2 11.9 %copy-start.1 = (bf16[4,256,128]{2,1,0:T(8,128)(2,1)S(1)}, bf16[4,256,128]{2,1,0:T(8,128)(2,1)}, u32[]{:S(2)}) copy-start(bf16[4,256,128]{2,1,0:T(8,128)(2,1)} %param.9) | copy-start | bytes 786436
  33.6 5.5 %copy-start.4 = (bf16[8,48,128]{2,1,0:T(8,128)(2,1)}, bf16[8,48,128]{2,1,0:T(8,128)(2,1)S(1)}, u32[]{:S(2)}) copy-start(bf16[8,48,128]{2,1,0:T(8,128)(2,1)S(1)} %all-to-all-done.2) | copy-start | bytes 294916
  33.6 40.4 %all-to-all-start = ((bf16[8,48,1024]{2,1,0:T(8,128)(2,1)}), bf16[8,48,1024]{2,1,0:T(8,128)(2,1)}, u32[]{:S(2)}, u32[]{:S(2)}) async-start(bf16[8,48,1024]{2,1,0:T(8,128)(2,1)} %broadcast_select_fusion), calls=%async_computation | async-start | bytes 1572864 | tf_op jit(solution)/shard_map/all_to_all | solution.py:52
  39.2 182.4 %all-reduce.3.cloned.1.call-start = ((), (), s32[]{:S(2)}) async-start(), calls=%async_computation.6 | async-start | bytes 1048576 | tf_op jit(solution)/shard_map/psum | solution.py:65
  41.2 204.6 %all-gather.2.cloned.1.call-start = ((), (), s32[]{:S(2)}) async-start(), calls=%async_computation.5 | async-start | bytes 2228224 | tf_op jit(solution)/shard_map/all_gather | solution.py:41
  41.7 239.5 %reduce-scatter.5.cloned.1.call-start = ((), (), s32[]{:S(2)}) async-start(), calls=%async_computation.8 | async-start | bytes 557056 | tf_op jit(solution)/shard_map/reduce_scatter | solution.py:89
  175.9 224.5 %reduce-scatter.3.cloned.1.call-start = ((), (), s32[]{:S(2)}) async-start(), calls=%async_computation.7 | async-start | bytes 4456448 | tf_op jit(solution)/shard_map/reduce_scatter | solution.py:88
  225.3 0.9 copy-start.2
  225.3 1.0 copy-start.3
  225.3 11.0 %copy-start.5 = (s32[256,1]{0,1:T(1,128)S(1)}, s32[256,1]{0,1:T(1,128)}, u32[]{:S(2)}) copy-start(s32[256,1]{0,1:T(1,128)} %param.11) | copy-start | bytes 3076
  227.3 17.6 %all-to-all-start.1 = ((bf16[8,48,128]{2,1,0:T(8,128)(2,1)}), bf16[8,48,128]{2,1,0:T(8,128)(2,1)S(1)}, u32[]{:S(2)}, u32[]{:S(2)}) async-start(bf16[8,48,128]{2,1,0:T(8,128)(2,1)} %copy.37), calls=%async_computation.1 | async-start | bytes 196608 | tf_op jit(solution)/shard_map/all_to_all | solution.py:83
Sparse Core Ops, SparseCore 0:
  43.9 177.6 all-reduce.2
Sparse Core Ops, SparseCore 1:
  45.8 83.3 all-gather.1
  176.0 105.1 reduce-scatter.4
  287.0 113.3 reduce-scatter.2
where the time goes:
time: 411 us; the launch traced here: 408 us
  waiting for transfers between devices  241 us (59%)
  blocking collectives  97.4 us (24%)
  starting transfers between devices  26.7 us (6%)
  between operations  15.8 us (4%)
  matrix products  13.7 us (3%)
  local copies, waits for them, and re-layouts  10.3 us (3%)
    reduce_scatter x1, waiting for transfers between devices, body(): lax.psum_scatter(part_a, 'fsdp', scatter_dimension=1, tiled=True)  119 us
    psum x1, blocking collectives, body(): lax.psum((hidden_partial, input_gradient_partial), 'tp')  97.4 us
    psum x1, waiting for transfers between devices, body(): lax.psum((hidden_partial, input_gradient_partial), 'tp')  45.6 us
    all_to_all x1, waiting for transfers between devices, body(): lax.all_to_all(send_x, 'ad', split_axis=0, concat_axis=0, tiled=True)  32.2 us
    reduce_scatter x1, waiting for transfers between devices, body(): lax.psum_scatter(up_weight_partial, 'fsdp', scatter_dimension=1, tiled=True)  30.7 us
    all_to_all x1, starting transfers between devices, body(): lax.all_to_all(send_dy, 'ad', split_axis=0, concat_axis=0, tiled=True)  12.1 us
    all_to_all x1, starting transfers between devices, body(): lax.all_to_all(adapter_update, 'ad', split_axis=0, concat_axis=0, tiled=T...  9.01 us
    all_to_all x1, waiting for transfers between devices, body(): lax.all_to_all(adapter_update, 'ad', split_axis=0, concat_axis=0, tiled=T...  8.54 us
  transfers between devices with their start and end apart: 7, of which 6 were waited for; matrix products, arithmetic and copies ran while one was open for 5% of the time, Pallas kernels for 0%

commit v1 on v0

v1 whole, which is shorter than its diff:
```python
import functools

import jax
import jax.numpy as jnp
from jax import lax
from jax.experimental import pallas as pl
from jax.experimental.pallas import tpu as pltpu
from jax.sharding import PartitionSpec as P

CAPD = 12
adapter_scale = 0.5
MESH = pl.DeviceIdType.MESH
F32 = jnp.float32
BF16 = jnp.bfloat16


def remote(src, dst, send_sem, recv_sem, device):
    return pltpu.make_async_remote_copy(
        src_ref=src, dst_ref=dst, send_sem=send_sem, recv_sem=recv_sem,
        device_id=device, device_id_type=MESH,
    )


def dot(a, b):
    return jnp.dot(a, b, preferred_element_type=F32)


def dot_nt(a, b):
    return lax.dot_general(a, b, (((1,), (1,)), ((), ())), preferred_element_type=F32)


def kernel(
    geo,
    dom_row_ref, dom_col_ref, x_hbm, w_hbm, down_hbm, up_hbm, dy_hbm,
    y_ref, ga_ref, gb_ref,
    xv, wg, av, bv, dyv,
    sdy, got_dy, sx, got_x,
    part_x, part_q, sum_v, zs, zr, full_v,
    bt, sa, sb, ra, rb, s2, r2, sgb, rgb,
    sret, ret,
    ld_sem, xs_sem, xr_sem, ds_sem, dr_sem, rs_sem, rr_sem, ws_sem, wr_sem,
    ps_sem, pr_sem, zs_sem, zr_sem, gs_sem, gr_sem, fs_sem, fr_sem,
    a1s_sem, a1r_sem, a2s_sem, a2r_sem, bs_sem, br_sem,
):
    NX, NY, NZH, NAD = geo
    NF = NX * NY
    NZ = NZH * NAD
    tokens = xv.shape[0]
    fw = av.shape[2]
    nd, rank = av.shape[0], av.shape[1]
    vw = bv.shape[2]
    wk = wg.shape[1]
    slots = nd * CAPD
    half = fw // 2
    rc = rank // NF

    fi = lax.axis_index("fsdp")
    ti = lax.axis_index("tp")
    ai = lax.axis_index("ad")
    yi, xi = lax.div(fi, NX), lax.rem(fi, NX)
    zh, core = lax.div(ti, 2), lax.rem(ti, 2)
    z = zh * NAD + ai
    sgn = 1 - 2 * core

    def zdev(k):
        zz = lax.rem(z + k + NZ, NZ)
        return lax.div(zz, NAD), lax.rem(zz, NAD)

    def fpeer(jy, jx):
        return lax.rem(yi + jy + NY, NY) * NX + lax.rem(xi + jx + NX, NX)

    def hpeer(j):
        return {"tp": lax.rem(zh + j + NZH, NZH) * 2 + core}

    partner = {"tp": zh * 2 + (1 - core)}

    ks = []
    for m in range(1, (NAD + 1) // 2):
        ks += [m, -m]
    if NAD > 1:
        ks.append((NAD // 2) * sgn)
    foff = [(j // NX, j % NX) for j in range(1, NF)]

    loads = [
        pltpu.make_async_copy(dy_hbm, dyv, ld_sem.at[0]),
        pltpu.make_async_copy(x_hbm, xv, ld_sem.at[1]),
        pltpu.make_async_copy(up_hbm, bv, ld_sem.at[2]),
        pltpu.make_async_copy(down_hbm, av, ld_sem.at[3]),
        pltpu.make_async_copy(w_hbm, wg.at[fi], ld_sem.at[4]),
    ]
    for c in loads:
        c.start()

    barrier = pltpu.get_barrier_semaphore()
    count = 0

    def greet(device):
        pl.semaphore_signal(barrier, inc=1, device_id=device, device_id_type=MESH)

    if NZH > 1:
        for j in (1, -1):
            greet(hpeer(j))
            count += 1
    for k in ks[:-1] + ([ks[-1], -ks[-1]] if ks else []):
        hh, aa = zdev(k)
        greet({"tp": hh * 2 + core, "ad": aa})
        count += 1
    for j in range(1, NAD):
        greet({"ad": lax.rem(ai + j, NAD)})
        count += 1
    for jy, jx in foff:
        greet({"fsdp": fpeer(jy, jx)})
        count += 1
    greet(partner)
    count += 1

    nall = nd * NAD
    dom_row = dom_row_ref[...].astype(F32)
    dom_col = dom_col_ref[...].astype(F32)
    ti0 = lax.broadcasted_iota(jnp.int32, (tokens, tokens), 0)
    ti1 = lax.broadcasted_iota(jnp.int32, (tokens, tokens), 1)
    oh_r = jnp.where(
        dom_row == lax.broadcasted_iota(jnp.int32, (nall, tokens), 0).astype(F32), 1.0, 0.0
    )
    oh_c = jnp.where(
        dom_col == lax.broadcasted_iota(jnp.int32, (tokens, nall), 1).astype(F32), 1.0, 0.0
    )
    before_r = dot(oh_r.astype(BF16), jnp.where(ti0 < ti1, 1.0, 0.0).astype(BF16))
    before_c = dot(jnp.where(ti1 < ti0, 1.0, 0.0).astype(BF16), oh_c.astype(BF16))
    place_r = dom_row * float(CAPD) + jnp.sum(before_r * oh_r, axis=0, keepdims=True)
    place_c = dom_col * float(CAPD) + jnp.sum(before_c * oh_c, axis=1, keepdims=True)

    def pick(dest):
        rows = lax.broadcasted_iota(jnp.int32, (slots, tokens), 0) + dest * slots
        return jnp.where(rows.astype(F32) == place_r, 1.0, 0.0).astype(BF16)

    loads[0].wait()
    dy_own = dyv[...]
    for j in range(NAD):
        aa = lax.rem(ai + j, NAD)
        out = dot(pick(aa), dy_own).astype(BF16)
        if j == 0:
            got_dy[ai] = out
        else:
            sdy[j] = out
    loads[1].wait()

    def packed(hh, aa):
        cols = pl.ds(pl.multiple_of((hh * 2 + core) * fw, fw), fw)
        return dot(pick(aa), xv[:, cols]).astype(BF16)

    for i, k in enumerate(ks):
        hh, aa = zdev(k)
        sx[i] = packed(hh, aa)

    pl.semaphore_wait(barrier, count)

    pending = []

    def go(copy):
        copy.start()
        pending.append(copy)

    for j in range(1, NAD):
        go(remote(sdy.at[j], got_dy.at[ai], ds_sem.at[j], dr_sem.at[j],
                  {"ad": lax.rem(ai + j, NAD)}))
    for i, k in enumerate(ks):
        hh, aa = zdev(k)
        go(remote(sx.at[i], got_x.at[ai], xs_sem.at[i], xr_sem.at[i],
                  {"tp": hh * 2 + core, "ad": aa}))
    for n, (jy, jx) in enumerate(foff):
        go(remote(w_hbm, wg.at[fi], ws_sem.at[n], wr_sem.at[n], {"fsdp": fpeer(jy, jx)}))

    got_x[ai] = packed(zh, ai)

    rowdom = lax.broadcasted_iota(jnp.int32, (NAD, slots, rank), 1)

    def own_rows(d):
        return (rowdom >= d * CAPD) & (rowdom < (d + 1) * CAPD)

    def share(which, value):
        for t in range(NAD):
            part_x[which, t % 2, t // 2] = value[t]
        go(remote(part_x.at[which, 1 - core], part_q.at[which],
                  ps_sem.at[which], pr_sem.at[which], partner))

    def wait_recv(dst, sem, device):
        remote(dst, dst, sem, sem, device).wait_recv()

    def ring_send(which, n, value, to):
        zs[which, n] = value.astype(BF16)
        go(remote(zs.at[which, n], zr.at[which, n], zs_sem.at[which, n], zr_sem.at[which, n],
                  hpeer(to)))

    def ring_open(which):
        wait_recv(part_q.at[which], pr_sem.at[which], partner)
        sum_v[which] = part_x[which, core] + part_q[which]
        if NZH > 1:
            ring_send(which, 0, sum_v[which, lax.rem(zh + 2, NZH)], sgn)
            ring_send(which, 2, sum_v[which, lax.rem(zh - sgn + NZH, NZH)], -sgn)

    def ring_mid(which):
        if NZH > 1:
            wait_recv(zr.at[which, 0], zr_sem.at[which, 0], hpeer(-sgn))
            own = sum_v[which, lax.rem(zh + sgn + NZH, NZH)]
            ring_send(which, 1, own + zr[which, 0].astype(F32), sgn)

    def chunk(j):
        return lax.rem(zh + j + NZH, NZH) * 2 + core

    def forward(which, n, j):
        at = full_v.at[which, chunk(j)]
        go(remote(at, at, fs_sem.at[which, n], fr_sem.at[which, n], partner))

    def gather_send(which, n, j, to):
        at = full_v.at[which, chunk(j)]
        go(remote(at, at, gs_sem.at[which, n], gr_sem.at[which, n], hpeer(to)))

    def ring_close(which, scale):
        total = sum_v[which, zh]
        if NZH > 1:
            wait_recv(zr.at[which, 1], zr_sem.at[which, 1], hpeer(-sgn))
            wait_recv(zr.at[which, 2], zr_sem.at[which, 2], hpeer(sgn))
            total = total + zr[which, 1].astype(F32) + zr[which, 2].astype(F32)
        full_v[which, chunk(0)] = (total * scale).astype(BF16)
        if NZH > 1:
            gather_send(which, 0, 0, sgn)
            gather_send(which, 1, 0, -sgn)
        forward(which, 0, 0)

    def gather_mid(which):
        if NZH > 1:
            wait_recv(full_v.at[which, chunk(-sgn)], gr_sem.at[which, 0], hpeer(-sgn))
            gather_send(which, 2, -sgn, sgn)
            forward(which, 1, -sgn)

    def gather_close(which):
        if NZH > 1:
            wait_recv(full_v.at[which, chunk(sgn)], gr_sem.at[which, 1], hpeer(sgn))
            forward(which, 2, sgn)
            wait_recv(full_v.at[which, chunk(2)], gr_sem.at[which, 2], hpeer(-sgn))
            forward(which, 3, 2)

    def gather_done(which):
        other = 1 - core
        for n, j in enumerate((0, sgn, -sgn, 2) if NZH > 1 else (0,)):
            at = full_v.at[which, lax.rem(zh + j + NZH, NZH) * 2 + other]
            wait_recv(at, fr_sem.at[which, n], partner)

    loads[2].wait()
    for j in range(1, NAD):
        src = lax.rem(ai - j + NAD, NAD)
        wait_recv(got_dy.at[src], dr_sem.at[j], {"ad": src})
    rows_dy = got_dy[...].reshape(NAD * slots, vw)
    acc = jnp.zeros((NAD, slots, rank), F32)
    for d in range(nd):
        acc = acc + jnp.where(
            own_rows(d), dot_nt(rows_dy, bv[d]).reshape(NAD, slots, rank), 0.0
        )
    share(0, acc)
    ring_open(0)

    loads[3].wait()
    for i, k in enumerate(ks):
        hh, aa = zdev(-k)
        wait_recv(got_x.at[aa], xr_sem.at[i], {"tp": hh * 2 + core, "ad": aa})
    rows_x = got_x[...].reshape(NAD * slots, fw)
    acc = jnp.zeros((NAD, slots, rank), F32)
    for d in range(nd):
        acc = acc + jnp.where(
            own_rows(d), dot_nt(rows_x, av[d]).reshape(NAD, slots, rank), 0.0
        )
    share(1, acc)
    ring_mid(0)
    ring_open(1)
    ring_close(0, adapter_scale)

    loads[4].wait()
    for n, (jy, jx) in enumerate(foff):
        src = fpeer(-jy, -jx)
        wait_recv(wg.at[src], wr_sem.at[n], {"fsdp": src})
    steps = 4 if NF % 4 == 0 else 1
    per = NF // steps

    gather_mid(0)
    ring_mid(1)
    gather_close(0)
    ring_close(1, 1.0)
    gather_done(0)

    lane = lax.broadcasted_iota(jnp.int32, (rank, NAD * slots), 1).astype(F32)
    lane = lane - float(slots) * jnp.floor((lane + 0.5) / float(slots))

    def lane_dom(d):
        return (lane >= float(d * CAPD)) & (lane < float((d + 1) * CAPD))

    back_t = full_v[0].reshape(NAD * slots, rank).astype(F32).T
    for d in range(nd):
        bt[d] = jnp.where(lane_dom(d), back_t, 0.0).astype(BF16)

    def part_a(h, dst, by_x):
        def one(d, _):
            res = dot(
                bt[d], got_x[:, :, h * half:(h + 1) * half].reshape(NAD * slots, half)
            ).astype(BF16).reshape(NF, rc, half)
            for f in range(NF):
                yy, xx = f // NX, f % NX
                if by_x:
                    dst[xx, yy, d] = res[f]
                else:
                    dst[yy, xx, d] = res[f]
            return 0

        lax.fori_loop(0, nd, one, 0)

    part_a(0, sa, True)
    for j in range(1, NX):
        xx = lax.rem(xi + j, NX)
        go(remote(sa.at[xx], ra.at[j], a1s_sem.at[0, j], a1r_sem.at[0, j],
                  {"fsdp": yi * NX + xx}))
    gather_mid(1)
    part_a(1, sb, False)
    for j in range(1, NY):
        yy = lax.rem(yi + j, NY)
        go(remote(sb.at[yy], rb.at[j], a1s_sem.at[1, j], a1r_sem.at[1, j],
                  {"fsdp": yy * NX + xi}))
    gather_close(1)

    base = jnp.zeros((tokens, vw), F32)
    base = lax.fori_loop(
        0, steps,
        lambda s, b: b + dot(
            xv[:, pl.ds(pl.multiple_of(s * (per * wk), per * wk), per * wk)],
            wg[pl.ds(s * per, per)].reshape(per * wk, vw)),
        base,
    )
    y_acc = base
    gather_done(1)

    hid = full_v[1].astype(F32)
    acc = jnp.zeros((NAD * slots, vw), F32)
    for d in range(nd):
        mine = jnp.where(own_rows(d), hid, 0.0).astype(BF16).reshape(NAD * slots, rank)
        acc = acc + dot(mine, bv[d])
    sret[...] = (adapter_scale * acc).astype(BF16).reshape(NAD, slots, vw)
    hid_t = hid.reshape(NAD * slots, rank).T
    rows_dy = got_dy[...].reshape(NAD * slots, vw)
    for j in range(1, NAD):
        aa = lax.rem(ai + j, NAD)
        go(remote(sret.at[aa], ret.at[ai], rs_sem.at[j], rr_sem.at[j], {"ad": aa}))
    ret[ai] = sret[ai]
    for d in range(nd):
        mine = jnp.where(lane_dom(d), hid_t, 0.0).astype(BF16)
        res = (adapter_scale * dot(mine, rows_dy)).astype(BF16).reshape(NF, rc, vw)
        for f in range(NF):
            sgb[f, d] = res[f]
    for n, (jy, jx) in enumerate(foff):
        dst = fpeer(jy, jx)
        go(remote(sgb.at[dst], rgb.at[n + 1], bs_sem.at[n], br_sem.at[n], {"fsdp": dst}))

    for j in range(1, NX):
        src = {"fsdp": yi * NX + lax.rem(xi - j + NX, NX)}
        wait_recv(ra.at[j], a1r_sem.at[0, j], src)
    for i in range(NY):
        yy = lax.rem(yi + i, NY)
        tot = sa[xi, yy].astype(F32)
        for j in range(1, NX):
            tot = tot + ra[j, yy].astype(F32)
        s2[0, i] = tot
    for i in range(1, NY):
        dst = {"fsdp": lax.rem(yi + i, NY) * NX + xi}
        go(remote(s2.at[0, i], r2.at[0, i], a2s_sem.at[0, i], a2r_sem.at[0, i], dst))
    for j in range(1, NY):
        src = {"fsdp": lax.rem(yi - j + NY, NY) * NX + xi}
        wait_recv(rb.at[j], a1r_sem.at[1, j], src)
    for i in range(NX):
        xx = lax.rem(xi + i, NX)
        tot = sb[yi, xx].astype(F32)
        for j in range(1, NY):
            tot = tot + rb[j, xx].astype(F32)
        s2[1, i] = tot
    for i in range(1, NX):
        dst = {"fsdp": yi * NX + lax.rem(xi + i, NX)}
        go(remote(s2.at[1, i], r2.at[1, i], a2s_sem.at[1, i], a2r_sem.at[1, i], dst))

    for j in range(1, NAD):
        src = lax.rem(ai - j + NAD, NAD)
        wait_recv(ret.at[src], rr_sem.at[j], {"ad": src})
    cols = lax.broadcasted_iota(jnp.int32, (tokens, NAD * slots), 1).astype(F32)
    unpick = jnp.where(cols == place_c, 1.0, 0.0).astype(BF16)
    y_acc = y_acc + dot(unpick, ret[...].reshape(NAD * slots, vw))
    y_ref[...] = y_acc.astype(BF16)

    tot = sgb[fi].astype(F32)
    for n, (jy, jx) in enumerate(foff):
        wait_recv(rgb.at[n + 1], br_sem.at[n], {"fsdp": fpeer(-jy, -jx)})
        tot = tot + rgb[n + 1].astype(F32)
    gb_ref[...] = tot
    for h, count_h in ((0, NY), (1, NX)):
        tot = s2[h, 0]
        for i in range(1, count_h):
            if h == 0:
                src = {"fsdp": lax.rem(yi - i + NY, NY) * NX + xi}
            else:
                src = {"fsdp": yi * NX + lax.rem(xi - i + NX, NX)}
            wait_recv(r2.at[h, i], a2r_sem.at[h, i], src)
            tot = tot + r2[h, i]
        ga_ref[:, :, h * half:(h + 1) * half] = tot

    for copy in pending:
        copy.wait_send()


def body(geo, x, w, down, up, dy, domain):
    NX, NY, NZH, NAD = geo
    NF = NX * NY
    tokens = x.shape[0]
    nd, rank, fw = down.shape
    vw = up.shape[2]
    slots = nd * CAPD
    half = fw // 2
    rc = rank // NF
    dom = domain[:, 0]
    V, D = pltpu.VMEM, pltpu.SemaphoreType.DMA
    nz = 4
    scratch = [
        V(x.shape, BF16), V((NF,) + w.shape, BF16), V(down.shape, BF16), V(up.shape, BF16),
        V(dy.shape, BF16),
        V((NAD, slots, vw), BF16), V((NAD, slots, vw), BF16),
        V((NAD, slots, fw), BF16), V((NAD, slots, fw), BF16),
        V((2, 2, NAD // 2, slots, rank), F32), V((2, NAD // 2, slots, rank), F32),
        V((2, NAD // 2, slots, rank), F32),
        V((2, 3, slots, rank), BF16), V((2, 3, slots, rank), BF16),
        V((2, NAD, slots, rank), BF16),
        V((nd, rank, NAD * slots), BF16),
        V((NX, NY, nd, rc, half), BF16), V((NY, NX, nd, rc, half), BF16),
        V((NX, NY, nd, rc, half), BF16), V((NY, NX, nd, rc, half), BF16),
        V((2, max(NX, NY), nd, rc, half), F32), V((2, max(NX, NY), nd, rc, half), F32),
        V((NF, nd, rc, vw), BF16), V((NF, nd, rc, vw), BF16),
        V((NAD, slots, vw), BF16), V((NAD, slots, vw), BF16),
        D((5,)), D((8,)), D((8,)), D((8,)), D((8,)), D((8,)), D((8,)), D((16,)), D((16,)),
        D((2,)), D((2,)), D((2, 3)), D((2, 3)), D((2, 3)), D((2, 3)), D((2, 4)), D((2, 4)),
        D((2, 4)), D((2, 4)), D((2, 4)), D((2, 4)), D((16,)), D((16,)),
    ]
    vm = pl.BlockSpec(memory_space=pltpu.VMEM)
    hbm = pl.BlockSpec(memory_space=pl.ANY)
    return pl.pallas_call(
        functools.partial(kernel, geo),
        out_shape=(
            jax.ShapeDtypeStruct((tokens, vw), BF16),
            jax.ShapeDtypeStruct((nd, rc, fw), F32),
            jax.ShapeDtypeStruct((nd, rc, vw), F32),
        ),
        in_specs=[vm, vm, hbm, hbm, hbm, hbm, hbm],
        out_specs=(vm, vm, vm),
        scratch_shapes=scratch,
        compiler_params=pltpu.CompilerParams(
            collective_id=0, has_side_effects=True, vmem_limit_bytes=60 * 1024 * 1024
        ),
        name="adapters",
    )(dom.reshape(1, tokens), domain, x, w, down, up, dy)


def geometry(mesh):
    side = 4 if mesh.shape["fsdp"] == 16 else 1
    return (side, mesh.shape["fsdp"] // side, mesh.shape["tp"] // 2, mesh.shape["ad"])


def solution(mesh):
    placed = (
        P(("fsdp", "ad"), None),
        P("fsdp", "tp"),
        P("ad", None, "tp"),
        P("ad", None, "tp"),
        P(("fsdp", "ad"), "tp"),
        P(("fsdp", "ad"), None),
    )
    return jax.shard_map(
        functools.partial(body, geometry(mesh)),
        mesh=mesh,
        in_specs=placed,
        out_specs=(P(("fsdp", "ad"), "tp"), P("ad", "fsdp", "tp"), P("ad", "fsdp", "tp")),
        check_vma=False,
    )
```

time: 411 us -> 116 us (0.28)
  the two profiles are of different devices: /device:TPU:33 before, /device:TPU:98 now
where the time goes in v1:
time: 116 us; the launch traced here: 115 us
  Pallas kernels  109 us (94%)
  local copies, waits for them, and re-layouts  5.99 us (5%)
    pallas_call x1, Pallas kernels, body(): pl.pallas_call(functools.partial(kernel, geo), out_shape=(jax.ShapeDtypeS...  109 us
    unnamed x4, local copies, waits for them, and re-layouts  5.99 us

profile of v1, /device:TPU:98, one launch (start us, length us, event | category | flops | bytes accessed | tf_op | source)
XLA Modules:
  0.0 115.2 jit_solution(15576948902903624890)
XLA Ops:
  0.6 1.5 %copy.9.dom_col_ref = s32[256,1]{1,0:T(8,128)} copy(s32[256,1]{0,1:T(1,128)} %param.11) | data formatting | bytes 2048 | tf_op args[5]
  2.1 108.6 %adapters.1 = (bf16[256,128]{1,0:T(8,128)(2,1)}, f32[4,16,1024]{2,1,0:T(8,128)}, f32[4,16,128]{2,1,0:T(8,128)}) custom-call(s32[1,256]{1,0:T(1,128)} %bitcast.1, s32[256,1]{1,0:T(8,128)} %copy.9.dom_col_ref, bf16[256,8192]{1,0:T(8,128)(2,1)} %x_hbm.1, bf16[512,128]{1,0:T(8,128)(2,1)} %w_hbm.1, bf16[4,256,1024]{2,1,0:T(8,128)(2,1)} %down_hbm.1, ...), custom_call_target="tpu_custom_call" | custom-call | tf_op jit(solution)/shard_map/adapters/pallas_call | solution.py:447
  110.7 1.5 %copy.13 = bf16[256,128]{1,0:T(8,128)(2,1)} copy(bf16[256,128]{1,0:T(8,128)(2,1)} %get-tuple-element.6) | data formatting | bytes 131072
  112.2 1.7 %copy.14 = f32[4,16,1024]{2,1,0:T(8,128)} copy(f32[4,16,1024]{2,1,0:T(8,128)} %get-tuple-element.7) | data formatting | bytes 524288
  113.8 1.4 %copy.15 = f32[4,16,128]{2,1,0:T(8,128)} copy(f32[4,16,128]{2,1,0:T(8,128)} %get-tuple-element.8) | data formatting | bytes 65536

commit v2 on v0

v2 whole, which is shorter than its diff:
```python
import functools

import jax
import jax.numpy as jnp
from jax import lax
from jax.experimental import pallas as pl
from jax.experimental.pallas import tpu as pltpu
from jax.sharding import PartitionSpec as P

CAPD = 12
adapter_scale = 0.5
EARLY = 4
VLIM = 61
MESH = pl.DeviceIdType.MESH
F32 = jnp.float32
BF16 = jnp.bfloat16


def remote(src, dst, send_sem, recv_sem, device):
    return pltpu.make_async_remote_copy(
        src_ref=src, dst_ref=dst, send_sem=send_sem, recv_sem=recv_sem,
        device_id=device, device_id_type=MESH,
    )


def dot(a, b):
    return jnp.dot(a, b, preferred_element_type=F32)


def dot_nt(a, b):
    return lax.dot_general(a, b, (((1,), (1,)), ((), ())), preferred_element_type=F32)


def kernel(
    geo,
    dom_ref, x_hbm, w_hbm, down_hbm, up_hbm, dy_hbm,
    y_ref, ga_ref, gb_ref,
    xv, wg, av, bv, dyv, base_v,
    sdy, got_dy, sx, got_x,
    part_x, part_q, sum_v, zs, zr, full_v,
    bt, st, rt, s2, r2, sgb, rgb,
    sret, ret,
    ld_sem, lx_sem, xs_sem, xr_sem, ds_sem, dr_sem, rs_sem, rr_sem, ws_sem, wr_sem,
    ps_sem, pr_sem, zs_sem, zr_sem, gs_sem, gr_sem, fs_sem, fr_sem,
    a1s_sem, a1r_sem, a2s_sem, a2r_sem, bs_sem, br_sem,
):
    NX, NZH, NAD = geo
    NF = NX * NX
    NZ = NZH * NAD
    NT = 2 * NZH
    tokens = xv.shape[1]
    fw = av.shape[2]
    nd, rank = av.shape[0], av.shape[1]
    vw = bv.shape[2]
    wk = wg.shape[1]
    slots = nd * CAPD
    half = fw // 2
    rc = rank // NF

    fi = lax.axis_index("fsdp")
    ti = lax.axis_index("tp")
    ai = lax.axis_index("ad")
    yi, xi = lax.div(fi, NX), lax.rem(fi, NX)
    zh, core = lax.div(ti, 2), lax.rem(ti, 2)
    z = zh * NAD + ai
    sgn = 1 - 2 * core
    other = 1 - core

    def zdev(k):
        zz = lax.rem(z + k + NZ, NZ)
        return lax.div(zz, NAD), lax.rem(zz, NAD)

    def near(k):
        return lax.rem(ai + k + NAD, NAD)

    def fpeer(jy, jx):
        return lax.rem(yi + jy + NX, NX) * NX + lax.rem(xi + jx + NX, NX)

    def hrow(j):
        return lax.rem(zh + j + NZH, NZH)

    def hpeer(j):
        return {"tp": hrow(j) * 2 + core}

    partner = {"tp": zh * 2 + other}

    ks = [0, (NAD // 2) * sgn]
    for m in range(NAD // 2 - 1, 0, -1):
        ks += [m, -m]
    groups = NAD // 2
    foff = [(j // NX, j % NX) for j in range(1, NF)]

    load_dy = pltpu.make_async_copy(dy_hbm, dyv, ld_sem.at[0])
    load_up = pltpu.make_async_copy(up_hbm, bv, ld_sem.at[1])
    load_down = pltpu.make_async_copy(down_hbm, av, ld_sem.at[2])
    load_w = pltpu.make_async_copy(w_hbm, wg.at[fi], ld_sem.at[3])
    load_dy.start()
    load_x = []
    for n in range(NT):
        blk = hrow((0, 1, -1, 2)[n // 2]) * 2 + (core if n % 2 == 0 else other)
        load_x.append((blk, n))
    load_x = load_x[0::2] + load_x[1::2]
    load_x = [
        pltpu.make_async_copy(
            x_hbm.at[:, pl.ds(pl.multiple_of(blk * fw, fw), fw)], xv.at[blk], lx_sem.at[n])
        for blk, n in load_x
    ]
    for c in load_x[:3]:
        c.start()
    load_up.start()
    load_down.start()
    load_w.start()
    for c in load_x[3:]:
        c.start()

    barrier = pltpu.get_barrier_semaphore()
    count = 0

    def greet(device):
        pl.semaphore_signal(barrier, inc=1, device_id=device, device_id_type=MESH)

    for j in (1, -1):
        greet(hpeer(j))
        count += 1
    for k in ks[1:] + [-ks[1]]:
        hh, aa = zdev(k)
        greet({"tp": hh * 2 + core, "ad": aa})
        count += 1
    for j in range(1, NAD):
        greet({"ad": lax.rem(ai + j, NAD)})
        count += 1
    for jy, jx in foff:
        greet({"fsdp": fpeer(jy, jx)})
        count += 1
    greet(partner)
    count += 1

    nall = nd * NAD
    dom_row = dom_ref[...].astype(F32)
    ti0 = lax.broadcasted_iota(jnp.int32, (tokens, tokens), 0)
    ti1 = lax.broadcasted_iota(jnp.int32, (tokens, tokens), 1)
    oh_r = jnp.where(
        dom_row == lax.broadcasted_iota(jnp.int32, (nall, tokens), 0).astype(F32), 1.0, 0.0
    )
    before_r = dot(oh_r.astype(BF16), jnp.where(ti0 < ti1, 1.0, 0.0).astype(BF16))
    place_r = dom_row * float(CAPD) + jnp.sum(before_r * oh_r, axis=0, keepdims=True)

    def pick(dest):
        rows = lax.broadcasted_iota(jnp.int32, (slots, tokens), 0) + dest * slots
        return jnp.where(rows.astype(F32) == place_r, 1.0, 0.0).astype(BF16)

    pending = []

    def go(copy):
        copy.start()
        pending.append(copy)

    load_dy.wait()
    dy_own = dyv[...]
    for i, k in enumerate(ks):
        out = dot(pick(near(k)), dy_own).astype(BF16)
        if i == 0:
            got_dy[0] = out
        else:
            sdy[i] = out
    for c in load_x[:3]:
        c.wait()

    def packed(k):
        hh, aa = zdev(k)
        return dot(pick(aa), xv[hh * 2 + core]).astype(BF16)

    def x_send(i):
        hh, aa = zdev(ks[i])
        go(remote(sx.at[i], got_x.at[i], xs_sem.at[i], xr_sem.at[i],
                  {"tp": hh * 2 + core, "ad": aa}))

    sx[1] = packed(ks[1])
    pl.semaphore_wait(barrier, count)

    for i in range(1, NAD):
        go(remote(sdy.at[i], got_dy.at[i], ds_sem.at[i], dr_sem.at[i], {"ad": near(ks[i])}))
    x_send(1)
    for i in range(2, 4):
        sx[i] = packed(ks[i])
    for i in range(2, 4):
        x_send(i)
    for n, (jy, jx) in enumerate(foff):
        go(remote(w_hbm, wg.at[fi], ws_sem.at[n], wr_sem.at[n], {"fsdp": fpeer(jy, jx)}))
    for i in range(4, EARLY):
        sx[i] = packed(ks[i])
        x_send(i)

    rowdom = lax.broadcasted_iota(jnp.int32, (NAD, slots, rank), 1)

    def own_rows(d, n):
        return (rowdom[:n] >= d * CAPD) & (rowdom[:n] < (d + 1) * CAPD)

    def wait_recv(dst, sem, device):
        remote(dst, dst, sem, sem, device).wait_recv()

    def partial(rows, weight, n):
        acc = jnp.zeros((n, slots, rank), F32)
        for d in range(nd):
            acc = acc + jnp.where(
                own_rows(d, n), dot_nt(rows, weight[d]).reshape(n, slots, rank), 0.0
            )
        return acc

    def share(which, g, value):
        part_x[which, 0, g] = value[0]
        part_x[which, 1, g] = value[1]
        go(remote(part_x.at[which, other, g], part_q.at[which, g],
                  ps_sem.at[which, g], pr_sem.at[which, g], partner))

    def merge(which, g):
        wait_recv(part_q.at[which, g], pr_sem.at[which, g], partner)
        sum_v[which, g] = part_x[which, core, g] + part_q[which, g]

    def chunk(j):
        return hrow(j) * 2 + core

    ring = [[remote(zs.at[w, n], zr.at[w, n], zs_sem.at[w, n], zr_sem.at[w, n], hpeer(to))
             for n, to in enumerate((sgn, sgn, -sgn))] for w in range(2)]
    spread = [[remote(full_v.at[w, chunk(j)], full_v.at[w, chunk(j)], gs_sem.at[w, n],
                      gr_sem.at[w, n], hpeer(to))
               for n, (j, to) in enumerate(((0, sgn), (0, -sgn), (-sgn, sgn)))] for w in range(2)]
    across = [[remote(full_v.at[w, chunk(j)], full_v.at[w, chunk(j)], fs_sem.at[w, n],
                      fr_sem.at[w, n], partner)
               for n, j in enumerate((0, -sgn, sgn, 2))] for w in range(2)]
    for w in range(2):
        pending.extend(ring[w] + spread[w] + across[w])

    def ring_first(which):
        zs[which, 0] = sum_v[which, hrow(2)].astype(BF16)
        ring[which][0].start()

    def ring_side(which):
        zs[which, 2] = sum_v[which, hrow(-sgn)].astype(BF16)
        ring[which][2].start()

    def ring_mid(which):
        wait_recv(zr.at[which, 0], zr_sem.at[which, 0], hpeer(-sgn))
        zs[which, 1] = (sum_v[which, hrow(sgn)] + zr[which, 0].astype(F32)).astype(BF16)
        ring[which][1].start()

    def ring_close(which, scale):
        wait_recv(zr.at[which, 2], zr_sem.at[which, 2], hpeer(sgn))
        wait_recv(zr.at[which, 1], zr_sem.at[which, 1], hpeer(-sgn))
        total = sum_v[which, zh] + zr[which, 1].astype(F32) + zr[which, 2].astype(F32)
        full_v[which, chunk(0)] = (total * scale).astype(BF16)
        spread[which][0].start()
        spread[which][1].start()
        across[which][0].start()

    def gather_mid(which):
        wait_recv(full_v.at[which, chunk(-sgn)], gr_sem.at[which, 0], hpeer(-sgn))
        spread[which][2].start()
        across[which][1].start()

    def gather_side(which):
        wait_recv(full_v.at[which, chunk(sgn)], gr_sem.at[which, 1], hpeer(sgn))
        across[which][2].start()

    def gather_close(which):
        wait_recv(full_v.at[which, chunk(2)], gr_sem.at[which, 2], hpeer(-sgn))
        across[which][3].start()

    def gather_done(which):
        for n, j in enumerate((0, sgn, -sgn, 2)):
            wait_recv(full_v.at[which, hrow(j) * 2 + other], fr_sem.at[which, n], partner)

    def at_row(g, j, step):
        @pl.when(hrow(j) == g)
        def _():
            step()

    def open_row(g):
        merge(1, g)
        at_row(g, 2, lambda: ring_first(1))
        at_row(g, -sgn, lambda: ring_side(1))

    def mid_row(g):
        at_row(g, sgn, lambda: ring_mid(1))

    def close_row(g):
        at_row(g, 0, lambda: ring_close(1, 1.0))

    def spread_row(g):
        at_row(g, -sgn, lambda: gather_mid(1))
        at_row(g, sgn, lambda: gather_side(1))

    def end_row(g):
        at_row(g, 2, lambda: gather_close(1))

    load_up.wait()
    for i in range(1, NAD):
        wait_recv(got_dy.at[i], dr_sem.at[i], {"ad": near(-ks[i])})
    value = partial(got_dy[...].reshape(NAD * slots, vw), bv, NAD)
    for g in range(groups):
        share(0, g, value[2 * g:2 * g + 2])
    for i in range(max(4, EARLY), NAD):
        sx[i] = packed(ks[i])
    for g in range(groups):
        merge(0, g)
    ring_first(0)
    ring_side(0)
    for i in range(max(4, EARLY), NAD):
        x_send(i)
    got_x[0] = packed(0)

    load_down.wait()

    def hidden_group(g):
        for i in (2 * g, 2 * g + 1):
            if i > 0:
                hh, aa = zdev(-ks[i])
                wait_recv(got_x.at[i], xr_sem.at[i], {"tp": hh * 2 + core, "ad": aa})
        share(1, g, partial(got_x[2 * g:2 * g + 2].reshape(2 * slots, fw), av, 2))

    per = NF // NT

    def base_step(n, _):
        rows = wg[pl.ds(n * per, per)].reshape(per * wk, vw)
        base_v[...] = base_v[...] + dot(xv[n], rows)
        return 0

    def base():
        for c in load_x[3:]:
            c.wait()
        load_w.wait()
        for n, (jy, jx) in enumerate(foff):
            src = fpeer(-jy, -jx)
            wait_recv(wg.at[src], wr_sem.at[n], {"fsdp": src})
        base_v[...] = jnp.zeros_like(base_v)
        lax.fori_loop(0, NT, base_step, 0)

    lane = lax.broadcasted_iota(jnp.int32, (rank, NAD * slots), 1).astype(F32)
    lane = lane - float(slots) * jnp.floor((lane + 0.5) / float(slots))

    def lane_dom(d):
        return (lane >= float(d * CAPD)) & (lane < float((d + 1) * CAPD))

    def prepare_a():
        back_t = full_v[0].reshape(NAD * slots, rank).astype(F32).T
        for d in range(nd):
            bt[d] = jnp.where(lane_dom(d), back_t, 0.0).astype(BF16)

    pairs = nd // 2
    line = (xi, yi)

    def axis_peer(h, j):
        if h == 0:
            return {"fsdp": fpeer(0, j)}
        return {"fsdp": fpeer(j, 0)}

    def part_a(h, p):
        def one(e, _):
            res = dot(
                bt[p * 2 + e], got_x[:, :, h * half:(h + 1) * half].reshape(NAD * slots, half)
            ).astype(BF16).reshape(NF, rc, half)
            for f in range(NF):
                yx = (f // NX, f % NX)
                st[h, p, yx[1 - h], yx[h], e] = res[f]
            return 0

        lax.fori_loop(0, 2, one, 0)
        for j in range(1, NX):
            go(remote(st.at[h, p, lax.rem(line[h] + j, NX)], rt.at[h, p, j],
                      a1s_sem.at[h, p, j], a1r_sem.at[h, p, j], axis_peer(h, j)))

    def fold_a(h, p):
        for j in range(1, NX):
            wait_recv(rt.at[h, p, j], a1r_sem.at[h, p, j], axis_peer(h, -j))
        for i in range(NX):
            at = lax.rem(line[1 - h] + i, NX)
            tot = st[h, p, line[h], at].astype(F32)
            for j in range(1, NX):
                tot = tot + rt[h, p, j, at].astype(F32)
            s2[h, p, i] = tot
        for i in range(1, NX):
            go(remote(s2.at[h, p, i], r2.at[h, p, i], a2s_sem.at[h, p, i], a2r_sem.at[h, p, i],
                      axis_peer(1 - h, i)))

    pieces = [(h, p) for p in range(pairs) for h in range(2)]
    hidden_group(0)
    open_row(0)
    hidden_group(1)
    open_row(1)
    ring_mid(0)
    hidden_group(2)
    open_row(2)
    hidden_group(3)
    open_row(3)
    ring_close(0, adapter_scale)
    mid_row(0)
    mid_row(1)
    mid_row(2)
    mid_row(3)
    gather_mid(0)
    gather_side(0)
    base()
    close_row(0)
    close_row(1)
    close_row(2)
    close_row(3)
    gather_close(0)
    gather_done(0)
    prepare_a()
    part_a(*pieces[0])
    part_a(*pieces[1])
    spread_row(0)
    spread_row(1)
    spread_row(2)
    spread_row(3)
    part_a(*pieces[2])
    part_a(*pieces[3])
    fold_a(*pieces[0])
    fold_a(*pieces[1])
    end_row(0)
    end_row(1)
    end_row(2)
    end_row(3)
    gather_done(1)

    hid = full_v[1].astype(F32)
    acc = jnp.zeros((NAD * slots, vw), F32)
    for d in range(nd):
        mine = jnp.where(own_rows(d, NAD), hid, 0.0).astype(BF16).reshape(NAD * slots, rank)
        acc = acc + dot(mine, bv[d])
    sret[...] = (adapter_scale * acc).astype(BF16).reshape(NAD, slots, vw)
    hid_t = hid.reshape(NAD * slots, rank).T
    for i in range(1, NAD):
        go(remote(sret.at[i], ret.at[i], rs_sem.at[i], rr_sem.at[i], {"ad": near(-ks[i])}))
    ret[0] = sret[0]
    rows_dy = got_dy[...].reshape(NAD * slots, vw)
    for d in range(nd):
        mine = jnp.where(lane_dom(d), hid_t, 0.0).astype(BF16)
        res = (adapter_scale * dot(mine, rows_dy)).astype(BF16).reshape(NF, rc, vw)
        for f in range(NF):
            sgb[f, d] = res[f]
    for n, (jy, jx) in enumerate(foff):
        dst = fpeer(jy, jx)
        go(remote(sgb.at[dst], rgb.at[n + 1], bs_sem.at[n], br_sem.at[n], {"fsdp": dst}))
    fold_a(*pieces[2])
    fold_a(*pieces[3])

    place_c = jnp.broadcast_to(place_r, (128, tokens)).T[:, 0:1]
    col = lax.broadcasted_iota(jnp.int32, (1, NAD * slots), 1)
    ident = jnp.zeros((1, NAD * slots), jnp.int32)
    for i, k in enumerate(ks):
        inside = (col >= i * slots) & (col < (i + 1) * slots)
        ident = jnp.where(inside, col + (near(k) - i) * slots, ident)
    unpick = jnp.where(ident.astype(F32) == place_c, 1.0, 0.0).astype(BF16)
    for i in range(1, NAD):
        wait_recv(ret.at[i], rr_sem.at[i], {"ad": near(ks[i])})
    y_ref[...] = (base_v[...] + dot(unpick, ret[...].reshape(NAD * slots, vw))).astype(BF16)

    tot = sgb[fi].astype(F32)
    for n, (jy, jx) in enumerate(foff):
        wait_recv(rgb.at[n + 1], br_sem.at[n], {"fsdp": fpeer(-jy, -jx)})
        tot = tot + rgb[n + 1].astype(F32)
    gb_ref[...] = tot
    for h, p in pieces:
        tot = s2[h, p, 0]
        for i in range(1, NX):
            wait_recv(r2.at[h, p, i], a2r_sem.at[h, p, i], axis_peer(1 - h, -i))
            tot = tot + r2[h, p, i]
        ga_ref[2 * p:2 * p + 2, :, h * half:(h + 1) * half] = tot

    for copy in pending:
        copy.wait_send()


def finish(y_in, ga_in, gb_in, y_ref, ga_ref, gb_ref):
    y_ref[...] = y_in[...]
    ga_ref[...] = ga_in[...]
    gb_ref[...] = gb_in[...]


def body(geo, x, w, down, up, dy, domain):
    NX, NZH, NAD = geo
    NF = NX * NX
    NT = 2 * NZH
    tokens = x.shape[0]
    nd, rank, fw = down.shape
    vw = up.shape[2]
    slots = nd * CAPD
    half = fw // 2
    rc = rank // NF
    pairs = nd // 2
    V, D = pltpu.VMEM, pltpu.SemaphoreType.DMA
    scratch = [
        V((NT, tokens, fw), BF16), V((NF,) + w.shape, BF16), V(down.shape, BF16),
        V(up.shape, BF16), V(dy.shape, BF16), V((tokens, vw), F32),
        V((NAD, slots, vw), BF16), V((NAD, slots, vw), BF16),
        V((NAD, slots, fw), BF16), V((NAD, slots, fw), BF16),
        V((2, 2, NZH, slots, rank), F32), V((2, NZH, slots, rank), F32),
        V((2, NZH, slots, rank), F32),
        V((2, 3, slots, rank), BF16), V((2, 3, slots, rank), BF16),
        V((2, NAD, slots, rank), BF16),
        V((nd, rank, NAD * slots), BF16),
        V((2, pairs, NX, NX, 2, rc, half), BF16), V((2, pairs, NX, NX, 2, rc, half), BF16),
        V((2, pairs, NX, 2, rc, half), F32), V((2, pairs, NX, 2, rc, half), F32),
        V((NF, nd, rc, vw), BF16), V((NF, nd, rc, vw), BF16),
        V((NAD, slots, vw), BF16), V((NAD, slots, vw), BF16),
        D((4,)), D((NT,)),
        D((NAD,)), D((NAD,)), D((NAD,)), D((NAD,)), D((NAD,)), D((NAD,)), D((NF,)), D((NF,)),
        D((2, NZH)), D((2, NZH)), D((2, 3)), D((2, 3)), D((2, 3)), D((2, 3)), D((2, 4)), D((2, 4)),
        D((2, pairs, NX)), D((2, pairs, NX)), D((2, pairs, NX)), D((2, pairs, NX)),
        D((NF,)), D((NF,)),
    ]
    vm = pl.BlockSpec(memory_space=pltpu.VMEM)
    hbm = pl.BlockSpec(memory_space=pltpu.HBM)
    shapes = (
        jax.ShapeDtypeStruct((tokens, vw), BF16),
        jax.ShapeDtypeStruct((nd, rc, fw), F32),
        jax.ShapeDtypeStruct((nd, rc, vw), F32),
    )
    results = pl.pallas_call(
        functools.partial(kernel, geo),
        out_shape=shapes,
        in_specs=[vm, hbm, hbm, hbm, hbm, hbm],
        out_specs=(vm, vm, vm),
        scratch_shapes=scratch,
        compiler_params=pltpu.CompilerParams(
            collective_id=0, has_side_effects=True, vmem_limit_bytes=VLIM * 1024 * 1024
        ),
        name="adapters",
    )(domain.reshape(1, tokens), x, w, down, up, dy)
    return tuple(
        pl.pallas_call(
            finish, out_shape=shapes, in_specs=[vm, vm, vm], out_specs=(vm, vm, vm),
            compiler_params=pltpu.CompilerParams(vmem_limit_bytes=8 * 1024 * 1024),
            name="finish",
        )(*results)
    )


def geometry(mesh):
    return (4, mesh.shape["tp"] // 2, mesh.shape["ad"])


def solution(mesh):
    placed = (
        P(("fsdp", "ad"), None),
        P("fsdp", "tp"),
        P("ad", None, "tp"),
        P("ad", None, "tp"),
        P(("fsdp", "ad"), "tp"),
        P(("fsdp", "ad"), None),
    )
    return jax.shard_map(
        functools.partial(body, geometry(mesh)),
        mesh=mesh,
        in_specs=placed,
        out_specs=(P(("fsdp", "ad"), "tp"), P("ad", "fsdp", "tp"), P("ad", "fsdp", "tp")),
        check_vma=False,
    )
```

time: 411 us -> 108 us (0.26)
  the two profiles are of different devices: /device:TPU:33 before, /device:TPU:81 now
where the time goes in v2:
time: 108 us
  Pallas kernels  104 us (96%)
  local copies, waits for them, and re-layouts  2.54 us (2%)
    pallas_call x1, Pallas kernels, body(): pl.pallas_call(functools.partial(kernel, geo), out_shape=shapes, in_specs...  104 us
    unnamed x6, local copies, waits for them, and re-layouts  2.54 us

profile of v2, /device:TPU:81, one launch (start us, length us, event | category | flops | bytes accessed | tf_op | source)
XLA Modules:
  0.0 107.5 jit_solution(8022257668891704995)
XLA Ops:
  0.6 103.6 %adapters.1 = (bf16[256,128]{1,0:T(8,128)(2,1)}, f32[4,16,1024]{2,1,0:T(8,128)}, f32[4,16,128]{2,1,0:T(8,128)}) custom-call(s32[1,256]{1,0:T(1,128)} %bitcast.1, bf16[256,8192]{1,0:T(8,128)(2,1)} %x_hbm.1, bf16[512,128]{1,0:T(8,128)(2,1)} %w_hbm.1, bf16[4,256,1024]{2,1,0:T(8,128)(2,1)} %down_hbm.1, bf16[4,256,128]{2,1,0:T(8,128)(2,1)} %up_hbm.1, ...), custom_call_target="tpu_custom_call" | custom-call | tf_op jit(solution)/shard_map/adapters/pallas_call | solution.py:520
  104.2 0.0 copy-start
  104.2 0.9 copy-done
  105.2 0.0 copy-start.1
  105.2 0.8 copy-done.1
  106.0 0.0 copy-start.2
  106.0 0.8 copy-done.2
  106.8 0.7 finish.1
Async XLA Ops:
  104.2 1.0 copy-start
  105.2 0.8 copy-start.1
  106.0 0.8 copy-start.2

commit v3 on v2

--- a/solution.py
+++ b/solution.py
@@ -10,7 +10,7 @@
 CAPD = 12
 adapter_scale = 0.5
 EARLY = 4
-VLIM = 61
+VLIM = 63
 MESH = pl.DeviceIdType.MESH
 F32 = jnp.float32
 BF16 = jnp.bfloat16
@@ -472,10 +472,17 @@
         copy.wait_send()
 
 
-def finish(y_in, ga_in, gb_in, y_ref, ga_ref, gb_ref):
-    y_ref[...] = y_in[...]
-    ga_ref[...] = ga_in[...]
-    gb_ref[...] = gb_in[...]
+def finish(y_in, ga_in, gb_in, y_ref, ga_ref, gb_ref, yv, gav, gbv, in_sem, out_sem):
+    stages = ((y_in, yv, y_ref), (ga_in, gav, ga_ref), (gb_in, gbv, gb_ref))
+    into = [pltpu.make_async_copy(a, v, in_sem.at[n]) for n, (a, v, _) in enumerate(stages)]
+    out = [pltpu.make_async_copy(v, o, out_sem.at[n]) for n, (_, v, o) in enumerate(stages)]
+    for c in into:
+        c.start()
+    for c, o in zip(into, out):
+        c.wait()
+        o.start()
+    for o in out:
+        o.wait()
 
 
 def body(geo, x, w, down, up, dy, domain):
@@ -530,8 +537,9 @@
     )(domain.reshape(1, tokens), x, w, down, up, dy)
     return tuple(
         pl.pallas_call(
-            finish, out_shape=shapes, in_specs=[vm, vm, vm], out_specs=(vm, vm, vm),
-            compiler_params=pltpu.CompilerParams(vmem_limit_bytes=8 * 1024 * 1024),
+            finish, out_shape=shapes, in_specs=[hbm] * 3, out_specs=(hbm,) * 3,
+            scratch_shapes=[V(t.shape, t.dtype) for t in shapes] + [D((3,)), D((3,))],
+            compiler_params=pltpu.CompilerParams(vmem_limit_bytes=VLIM * 1024 * 1024),
             name="finish",
         )(*results)
     )

time: 108 us -> 106 us (0.981)
  local copies, waits for them, and re-layouts: 2.54 us -> 0 us
    unnamed x6 -> x0, local copies, waits for them, and re-layouts: 2.54 us -> none
where the time goes in v3:
time: 106 us
  Pallas kernels  105 us (99%)
    pallas_call x1, Pallas kernels, body(): pl.pallas_call(functools.partial(kernel, geo), out_shape=shapes, in_specs...  104 us

profile of v3, /device:TPU:81, one launch (start us, length us, event | category | flops | bytes accessed | tf_op | source)
XLA Modules:
  0.0 106.0 jit_solution(160811237814187819)
XLA Ops:
  0.6 103.6 %adapters.1 = (bf16[256,128]{1,0:T(8,128)(2,1)}, f32[4,16,1024]{2,1,0:T(8,128)}, f32[4,16,128]{2,1,0:T(8,128)}) custom-call(s32[1,256]{1,0:T(1,128)} %bitcast.1, bf16[256,8192]{1,0:T(8,128)(2,1)} %x_hbm.1, bf16[512,128]{1,0:T(8,128)(2,1)} %w_hbm.1, bf16[4,256,1024]{2,1,0:T(8,128)(2,1)} %down_hbm.1, bf16[4,256,128]{2,1,0:T(8,128)(2,1)} %up_hbm.1, ...), custom_call_target="tpu_custom_call" | custom-call | tf_op jit(solution)/shard_map/adapters/pallas_call | solution.py:527
  104.2 1.7 %finish.1 = (bf16[256,128]{1,0:T(8,128)(2,1)}, f32[4,16,1024]{2,1,0:T(8,128)}, f32[4,16,128]{2,1,0:T(8,128)}) custom-call(bf16[256,128]{1,0:T(8,128)(2,1)} %get-tuple-element.6.y_in, f32[4,16,1024]{2,1,0:T(8,128)} %get-tuple-element.7.ga_in, f32[4,16,128]{2,1,0:T(8,128)} %get-tuple-element.8.gb_in), custom_call_target="tpu_custom_call" | custom-call | tf_op jit(solution)/shard_map/finish/pallas_call | solution.py:539

commit v4 on v3

--- a/solution.py
+++ b/solution.py
@@ -85,7 +85,7 @@
     partner = {"tp": zh * 2 + other}
 
     ks = [0, (NAD // 2) * sgn]
-    for m in range(NAD // 2 - 1, 0, -1):
+    for m in (2, 3, 1):
         ks += [m, -m]
     groups = NAD // 2
     foff = [(j // NX, j % NX) for j in range(1, NF)]

time: 106 us -> 105 us (level)
  the two profiles are of different devices: /device:TPU:81 before, /device:TPU:33 now
where the time goes in v4:
time: 105 us
  Pallas kernels  104 us (99%)
    pallas_call x1, Pallas kernels, body(): pl.pallas_call(functools.partial(kernel, geo), out_shape=shapes, in_specs...  102 us

profile of v4, /device:TPU:33, one launch (start us, length us, event | category | flops | bytes accessed | tf_op | source)
XLA Modules:
  0.0 104.8 jit_solution(2120764869533253065)
XLA Ops:
  0.6 102.5 %adapters.1 = (bf16[256,128]{1,0:T(8,128)(2,1)}, f32[4,16,1024]{2,1,0:T(8,128)}, f32[4,16,128]{2,1,0:T(8,128)}) custom-call(s32[1,256]{1,0:T(1,128)} %bitcast.1, bf16[256,8192]{1,0:T(8,128)(2,1)} %x_hbm.1, bf16[512,128]{1,0:T(8,128)(2,1)} %w_hbm.1, bf16[4,256,1024]{2,1,0:T(8,128)(2,1)} %down_hbm.1, bf16[4,256,128]{2,1,0:T(8,128)(2,1)} %up_hbm.1, ...), custom_call_target="tpu_custom_call" | custom-call | tf_op jit(solution)/shard_map/adapters/pallas_call | solution.py:527
  103.1 1.7 %finish.1 = (bf16[256,128]{1,0:T(8,128)(2,1)}, f32[4,16,1024]{2,1,0:T(8,128)}, f32[4,16,128]{2,1,0:T(8,128)}) custom-call(bf16[256,128]{1,0:T(8,128)(2,1)} %get-tuple-element.6.y_in, f32[4,16,1024]{2,1,0:T(8,128)} %get-tuple-element.7.ga_in, f32[4,16,128]{2,1,0:T(8,128)} %get-tuple-element.8.gb_in), custom_call_target="tpu_custom_call" | custom-call | tf_op jit(solution)/shard_map/finish/pallas_call | solution.py:539

commit v5 on v4

--- a/solution.py
+++ b/solution.py
@@ -432,6 +432,8 @@
     hid_t = hid.reshape(NAD * slots, rank).T
     for i in range(1, NAD):
         go(remote(sret.at[i], ret.at[i], rs_sem.at[i], rr_sem.at[i], {"ad": near(-ks[i])}))
+    fold_a(*pieces[2])
+    fold_a(*pieces[3])
     ret[0] = sret[0]
     rows_dy = got_dy[...].reshape(NAD * slots, vw)
     for d in range(nd):
@@ -442,8 +444,6 @@
     for n, (jy, jx) in enumerate(foff):
         dst = fpeer(jy, jx)
         go(remote(sgb.at[dst], rgb.at[n + 1], bs_sem.at[n], br_sem.at[n], {"fsdp": dst}))
-    fold_a(*pieces[2])
-    fold_a(*pieces[3])
 
     place_c = jnp.broadcast_to(place_r, (128, tokens)).T[:, 0:1]
     col = lax.broadcasted_iota(jnp.int32, (1, NAD * slots), 1)

time: 105 us -> 107 us (1.019)
  Pallas kernels: 104 us -> 106 us
    pallas_call x1, Pallas kernels: 102 us -> 104 us  [body(): pl.pallas_call(functools.partial(kernel, geo), out_shape=shapes, in_specs...]
where the time goes in v5:
time: 107 us
  Pallas kernels  106 us (99%)
    pallas_call x1, Pallas kernels, body(): pl.pallas_call(functools.partial(kernel, geo), out_shape=shapes, in_specs...  104 us

profile of v5, /device:TPU:33, one launch (start us, length us, event | category | flops | bytes accessed | tf_op | source)
XLA Modules:
  0.0 106.6 jit_solution(6968711735668451141)
XLA Ops:
  0.6 104.2 %adapters.1 = (bf16[256,128]{1,0:T(8,128)(2,1)}, f32[4,16,1024]{2,1,0:T(8,128)}, f32[4,16,128]{2,1,0:T(8,128)}) custom-call(s32[1,256]{1,0:T(1,128)} %bitcast.1, bf16[256,8192]{1,0:T(8,128)(2,1)} %x_hbm.1, bf16[512,128]{1,0:T(8,128)(2,1)} %w_hbm.1, bf16[4,256,1024]{2,1,0:T(8,128)(2,1)} %down_hbm.1, bf16[4,256,128]{2,1,0:T(8,128)(2,1)} %up_hbm.1, ...), custom_call_target="tpu_custom_call" | custom-call | tf_op jit(solution)/shard_map/adapters/pallas_call | solution.py:527
  104.8 1.7 %finish.1 = (bf16[256,128]{1,0:T(8,128)(2,1)}, f32[4,16,1024]{2,1,0:T(8,128)}, f32[4,16,128]{2,1,0:T(8,128)}) custom-call(bf16[256,128]{1,0:T(8,128)(2,1)} %get-tuple-element.6.y_in, f32[4,16,1024]{2,1,0:T(8,128)} %get-tuple-element.7.ga_in, f32[4,16,128]{2,1,0:T(8,128)} %get-tuple-element.8.gb_in), custom_call_target="tpu_custom_call" | custom-call | tf_op jit(solution)/shard_map/finish/pallas_call | solution.py:539
